TPU v7x, 32 devices: a whole 2x2x4 slice. The times are simulated.
32 devices in a mesh: lat: 8 (over y, x, core), lev: 4 (over z).
Axes of the slice: x: 2, y: 2, z: 4, core: 2. Of those that a mesh axis runs over, the one named last changes fastest.
Arguments:
- grid_adjoint: float32 [2, 96, 640, 1280], P(None, 'lev', 'lat'), may hold values from -6 to 6
- trajectory: bfloat16 [2, 96, 640, 1280], P(None, 'lev', 'lat'), may hold values from -5 to 5
- pair_order: int32 [320], replicated, may hold values from 0 to 319, each once
- legendre: bfloat16 [320, 640, 641], P('lat'), may hold values from -0.25 to 0.25
- modes: bfloat16 [96, 96], replicated, may hold values from -0.625 to 0.625
- rates: float32 [96], replicated, may hold values from 0.5 to 50
Outputs:
- grid_out: float32 [2, 96, 640, 1280], P(None, 'lev', 'lat')
Inputs may be any that keep to these rules, and one draw needn't show every extreme that they name: `pair_order`: A permutation: entry s names the pair k and 639 - k whose basis values are row s of legendre.
All inputs are finite; a program needn't handle non-finite values.
Results may differ from a plain program's by a relative error of at most 0.0068.
Values may be sent and summed in bfloat16 or wider, within the bound.
A program may use at most 192 MiB of HBM per device.

v0:
```python
import math
import jax
import jax.numpy as jnp
from jax import lax
from jax.sharding import PartitionSpec as P


def tables(length, number):
    row = lax.broadcasted_iota(jnp.int32, (length, 2 * number), 0)
    col = lax.broadcasted_iota(jnp.int32, (length, 2 * number), 1)
    wavenum = col % number
    phases = 2.0 * math.pi / length * (row * wavenum % length).astype(jnp.float32)
    forward = (jnp.where(col < number, jnp.cos(phases), -jnp.sin(phases)) / length).astype(
        jnp.bfloat16
    )
    inrow = lax.broadcasted_iota(jnp.int32, (2 * number, length), 0)
    position = lax.broadcasted_iota(jnp.int32, (2 * number, length), 1)
    inwave = inrow % number
    inphase = 2.0 * math.pi / length * (position * inwave % length).astype(jnp.float32)
    weights = jnp.where(inwave == 0, 1.0, 2.0).astype(jnp.float32)
    inverse = jnp.where(
        inrow < number, weights * jnp.cos(inphase), -weights * jnp.sin(inphase)
    ).astype(jnp.bfloat16)
    return (forward, inverse)


def degrees(waves_a, truncation):
    column = lax.broadcasted_iota(jnp.int32, (waves_a.shape[0], truncation + 1), 1)
    lower_part = column < (truncation - waves_a)[:, None]
    degree = jnp.where(lower_part, waves_a[:, None] + column, column - 1)
    degree_ratio = (degree * (degree + 1)).astype(jnp.float32) / float(
        truncation * (truncation + 1)
    )
    return (lower_part, degree_ratio)


def per_device(grid_adjoint, trajectory, pair_order, legendre, modes, rates):
    fields, levels, lat_rows, longitudes = grid_adjoint.shape
    wave_count = longitudes // 2
    slot_count = legendre.shape[0]
    lat_count = legendre.shape[1]
    primary = trajectory[0].astype(jnp.float32)
    coupling = trajectory[1].astype(jnp.float32)
    coupled = jnp.stack(
        [
            primary * grid_adjoint[0] + coupling * grid_adjoint[1],
            coupling * grid_adjoint[0] + primary * grid_adjoint[1],
        ]
    ).astype(jnp.bfloat16)
    forward, inverse = tables(longitudes, wave_count)
    fourier_local = jnp.dot(
        coupled.reshape(-1, longitudes), forward, preferred_element_type=jnp.float32
    )
    fourier_local = fourier_local.astype(jnp.bfloat16).reshape(
        fields, levels, lat_rows, 2, wave_count
    )
    column_order = jnp.stack([pair_order, wave_count - 1 - pair_order], axis=1).reshape(-1)
    permuted = jnp.take(fourier_local, column_order, axis=4)
    received_bands = lax.all_to_all(permuted, "lat", split_axis=4, concat_axis=2, tiled=True)
    grouped = received_bands.reshape(fields, levels, lat_count, 2, slot_count, 2)
    band_index = lax.axis_index("lat")
    local_waves = lax.dynamic_slice_in_dim(pair_order, band_index * slot_count, slot_count)
    lower_part, degree_ratio = degrees(local_waves, wave_count)
    products = jnp.einsum(
        "slj,fvlcsh->sfvchj", legendre, grouped, preferred_element_type=jnp.float32
    )
    lower_mask = lower_part[:, None, None, None, :]
    spectral = jnp.where(lower_mask, products[:, :, :, :, 0], products[:, :, :, :, 1])
    damped = spectral[:, 0] / (1.0 + 4.0 * degree_ratio * degree_ratio)[:, None, None, :]
    rounded = spectral[:, 1].astype(jnp.bfloat16)
    level_index = lax.axis_index("lev")
    lev_count = lax.axis_size("lev")
    flattened = jnp.transpose(rounded, (1, 0, 2, 3)).reshape(levels, -1)
    column_total = flattened.shape[1]
    column_width = -(-column_total // lev_count)
    padding = column_width * lev_count - column_total
    padded = jnp.pad(flattened, ((0, 0), (0, padding)))
    columns = lax.all_to_all(padded, "lev", split_axis=1, concat_axis=0, tiled=True)
    ratio_flat = jnp.broadcast_to(
        degree_ratio[:, None, :], (slot_count, 2, wave_count + 1)
    ).reshape(-1)
    ratio_flat = jnp.pad(ratio_flat, (0, padding))
    ratio_piece = lax.dynamic_slice_in_dim(ratio_flat, level_index * column_width, column_width)
    projected = jnp.einsum("km,kn->mn", modes, columns, preferred_element_type=jnp.float32)
    factor = 1.0 / (1.0 + rates[:, None] * ratio_piece[None, :])
    weighted = (projected * factor).astype(jnp.bfloat16)
    solved_columns = jnp.dot(modes, weighted, preferred_element_type=jnp.float32)
    returned_levels = lax.all_to_all(
        solved_columns.astype(jnp.bfloat16), "lev", split_axis=0, concat_axis=1, tiled=True
    ).astype(solved_columns.dtype)
    solved = returned_levels[:, :column_total].reshape(levels, slot_count, 2, wave_count + 1)
    solved = jnp.transpose(solved, (1, 0, 2, 3))
    updated = jnp.stack([damped, solved], axis=1).astype(jnp.bfloat16)
    zero_value = jnp.zeros((), jnp.bfloat16)
    halves = jnp.stack(
        [jnp.where(lower_mask, updated, zero_value), jnp.where(lower_mask, zero_value, updated)],
        axis=-2,
    )
    synthesised = jnp.einsum(
        "slj,sfvchj->fvlcsh", legendre, halves, preferred_element_type=jnp.float32
    )
    synthesised = synthesised.astype(jnp.bfloat16).reshape(
        fields, levels, lat_count, 2, slot_count * 2
    )
    returned = lax.all_to_all(synthesised, "lat", split_axis=2, concat_axis=4, tiled=True)
    inverse_order = (
        jnp.zeros((wave_count,), jnp.int32)
        .at[column_order]
        .set(jnp.arange(wave_count, dtype=jnp.int32))
    )
    natural = jnp.take(returned, inverse_order, axis=4)
    grid_out = jnp.dot(
        natural.reshape(-1, 2 * wave_count), inverse, preferred_element_type=jnp.float32
    )
    return grid_out.reshape(fields, levels, lat_rows, longitudes)


def solution(mesh):
    placed = (
        P(None, "lev", "lat", None),
        P(None, "lev", "lat", None),
        P(),
        P("lat", None, None),
        P(),
        P(),
    )
    return jax.shard_map(
        per_device,
        mesh=mesh,
        in_specs=placed,
        out_specs=P(None, "lev", "lat", None),
        check_vma=False,
    )
```

profile of v0, /device:TPU:0, one launch (start us, length us, event | category | flops | bytes accessed | tf_op | source)
XLA Modules:
  0.0 961.1 jit_solution(389869084658848675)
XLA Ops:
  1.8 14.9 %fusion.9 = (bf16[1,24,80,1280]{3,2,1,0:T(8,128)(2,1)}, bf16[1,24,80,1280]{3,2,1,0:T(8,128)(2,1)}) fusion(f32[2,24,80,1280]{3,2,1,0:T(8,128)} %param.8, bf16[2,24,80,1280]{3,2,1,0:T(8,128)(2,1)} %param.9), kind=kLoop, calls=%fused_computation.25 | loop fusion | flops 24576000 | bytes 39321600 | tf_op jit(solution)/shard_map/convert.8
  16.6 8.6 pad_maximum_fusion.1
  25.3 27.6 %multiply_convert_fusion.4 = bf16[1280,1280]{1,0:T(8,128)(2,1)S(1)} fusion(s32[1280]{0:T(1024)S(1)} %get-tuple-element.14, s32[1280]{0:T(1024)S(1)} %get-tuple-element.15, pred[1280]{0:T(1024)(128)(4,1)S(1)} %get-tuple-element.17, pred[1280]{0:T(1024)(128)(4,1)S(1)} %get-tuple-element.16), kind=kLoop, calls=%fused_computation.47.clone.clone.1 | loop fusion | flops 22937600 | bytes 3289600 | tf_op jit(solution)/shard_map/dot_general | solution.py:51
  52.9 19.0 %convolution_convert_fusion.1 = bf16[3840,1280]{1,0:T(8,128)(2,1)} fusion(bf16[3840,1280]{1,0:T(8,128)(2,1)} %bitcast.82, bf16[1280,1280]{1,0:T(8,128)(2,1)S(1)} %multiply_convert_fusion.4), kind=kOutput, calls=%fused_computation.14 | convolution fusion | flops 12587827200 | bytes 22937600 | tf_op jit(solution)/shard_map/dot_general | solution.py:51
  71.9 19.3 %reshape.233 = bf16[2,24,80,2,640]{4,3,2,1,0:T(2,128)(2,1)} reshape(bf16[3840,1280]{1,0:T(8,128)(2,1)} %convolution_convert_fusion.1) | data formatting | bytes 19660800 | tf_op jit(solution)/shard_map/reshape | solution.py:54
  91.2 25.9 %copy.64 = bf16[2,24,80,2,640]{2,1,3,0,4:T(8,128)(2,1)} copy(bf16[2,24,80,2,640]{4,3,2,1,0:T(2,128)(2,1)} %reshape.233) | data formatting | bytes 19660800 | tf_op jit(solution)/shard_map/reshape | solution.py:54
  117.1 25.2 %gather_fusion = bf16[640,2,24,80,2]{3,2,4,1,0:T(8,128)(2,1)} fusion(bf16[2,24,80,2,640]{2,1,3,0,4:T(8,128)(2,1)} %copy.64, s32[1024]{0:T(1024)S(1)} %pad_clamp_fusion.1), kind=kCustom, calls=%fused_computation.clone | custom fusion | bytes 19663360 | tf_op jit(solution)/shard_map/jit(_take)/gather | solution.py:58
  142.3 14.0 %select_bitcast_fusion.1 = bf16[2,24,80,2,640]{2,1,3,0,4:T(8,128)(2,1)} fusion(bf16[640,2,24,80,2]{3,2,4,1,0:T(8,128)(2,1)} %gather_fusion, pred[640]{0:T(1024)(128)(4,1)S(1)} %compare_and_fusion.1), kind=kLoop, calls=%fused_computation.9 | loop fusion | flops 4915200 | bytes 19661440 | tf_op jit(solution)/shard_map/jit(_take)/select_n | solution.py:58
  156.3 5.6 all-to-all-start
  162.8 172.5 %all-to-all-done = bf16[2,24,80,2,640]{2,1,3,0,4:T(8,128)(2,1)} async-done(((bf16[2,24,80,2,640]{2,1,3,0,4:T(8,128)(2,1)}), bf16[2,24,80,2,640]{2,1,3,0,4:T(8,128)(2,1)}, u32[]{:S(2)}, u32[]{:S(2)}) %all-to-all-start) | async-done | bytes 9830432 | tf_op jit(solution)/shard_map/all_to_all | solution.py:59
  335.4 27.2 %copy.104 = bf16[2,24,80,2,8,80]{2,4,1,5,3,0:T(8,128)(2,1)} copy(bf16[2,24,80,2,8,80]{2,1,3,0,5,4:T(8,128)(2,1)} %bitcast.2) | data formatting | bytes 19660800 | tf_op jit(solution)/shard_map/all_to_all | solution.py:59
  362.6 23.1 %reshape.235 = bf16[2,24,640,2,40,2]{2,1,5,4,3,0:T(8,128)(2,1)} reshape(bf16[2,24,8,80,2,80]{3,2,1,5,4,0:T(8,128)(2,1)} %bitcast.76) | data formatting | bytes 19660800 | tf_op jit(solution)/shard_map/reshape | solution.py:60
  385.6 29.7 %fusion.2 = f32[40,2,24,2,2,641]{5,2,4,3,1,0:T(8,128)} fusion(bf16[40,640,641,1,1,1]{1,0,2,5,4,3:T(8,128)(2,1)} %bitcast.79, bf16[2,24,640,2,40,2]{2,1,5,4,3,0:T(8,128)(2,1)} %reshape.235), kind=kOutput, calls=%fused_computation.5 | convolution fusion | flops 6301286400 | bytes 62341120 | tf_op jit(solution)/shard_map/slj,fvlcsh->sfvchj/dot_general | solution.py:64
  415.3 9.1 fusion.6
  424.5 4.5 copy-done.2
  438.8 15.4 %all-to-all-start.1 = ((bf16[24,4,12820]{2,0,1:T(8,128)(2,1)}), bf16[24,4,12820]{2,0,1:T(8,128)(2,1)S(1)}, u32[]{:S(2)}, u32[]{:S(2)}) async-start(bf16[24,4,12820]{2,0,1:T(8,128)(2,1)} %copy.70), calls=%async_computation.1 | async-start | bytes 4964352 | tf_op jit(solution)/shard_map/all_to_all | solution.py:78
  454.8 52.9 %all-to-all-done.1 = bf16[24,4,12820]{2,0,1:T(8,128)(2,1)S(1)} async-done(((bf16[24,4,12820]{2,0,1:T(8,128)(2,1)}), bf16[24,4,12820]{2,0,1:T(8,128)(2,1)S(1)}, u32[]{:S(2)}, u32[]{:S(2)}) %all-to-all-start.1) | async-done | bytes 2461472 | tf_op jit(solution)/shard_map/all_to_all | solution.py:78
  510.7 4.5 all-to-all-start.2
  518.7 52.7 %all-to-all-done.2 = bf16[4,24,12820]{2,1,0:T(8,128)(2,1)} async-done(((bf16[4,24,12820]{2,1,0:T(8,128)(2,1)}), bf16[4,24,12820]{2,1,0:T(8,128)(2,1)}, u32[]{:S(2)}, u32[]{:S(2)}) %all-to-all-start.2) | async-done | bytes 2461472 | tf_op jit(solution)/shard_map/all_to_all | solution.py:88
  575.5 10.8 %convert_element_type.92 = bf16[24,40,2,641]{3,2,1,0:T(2,128)(2,1)} reshape(bf16[24,4,12820]{2,1,0:T(4,128)(2,1)} %copy.71) | data formatting | bytes 4922880 | tf_op jit(solution)/shard_map/convert_element_type | solution.py:90
  591.3 22.3 %convert_bitcast_fusion = bf16[2,24,640,2,40,2]{2,1,5,3,0,4:T(8,128)(2,1)} fusion(bf16[40,640,641,1,1,1]{1,0,2,5,4,3:T(8,128)(2,1)} %bitcast.80, bf16[40,2,24,2,1,641]{5,2,3,0,4,1:T(8,128)(2,1)S(1)} %get-tuple-element.11, bf16[40,2,24,2,1,641]{5,2,3,0,4,1:T(8,128)(2,1)S(1)} %get-tuple-element.10), kind=kOutput, calls=%fused_computation.31 | convolution fusion | flops 6311124480 | bytes 52495360 | tf_op jit(solution)/shard_map/slj,sfvchj->fvlcsh/dot_general | solution.py:99
  613.6 8.4 copy.75
  622.0 20.1 %copy.76 = bf16[2,24,640,2,80]{4,1,3,0,2:T(8,128)(2,1)} copy(bf16[2,24,640,2,80]{2,1,4,3,0:T(8,128)(2,1)} %bitcast.78) | data formatting | bytes 19660800 | tf_op jit(solution)/shard_map/reshape | solution.py:102
  642.2 6.0 all-to-all-start.3
  652.5 30.0 %fusion.83 = bf16[1280,1280,1,1]{1,0,3,2:T(8,128)(2,1)S(1)} fusion(s32[1280]{0:T(1024)S(1)} %copy-done.6, s32[1280]{0:T(1024)S(1)} %copy-done.8, pred[1280]{0:T(1024)(128)(4,1)S(1)} %copy-done.12, pred[1280]{0:T(1024)(128)(4,1)S(1)} %copy-done.10), kind=kLoop, calls=%fused_computation.59.clone.clone.1 | loop fusion | flops 27852800 | bytes 3289600 | tf_op jit(solution)/shard_map/dot_general | solution.py:112
  682.5 138.4 %all-to-all-done.3 = bf16[2,24,640,2,80]{4,1,3,0,2:T(8,128)(2,1)} async-done(((bf16[2,24,640,2,80]{4,1,3,0,2:T(8,128)(2,1)}), bf16[2,24,640,2,80]{4,1,3,0,2:T(8,128)(2,1)}, u32[]{:S(2)}, u32[]{:S(2)}) %all-to-all-start.3) | async-done | bytes 9830432 | tf_op jit(solution)/shard_map/all_to_all | solution.py:105
  820.9 33.7 %copy.87 = bf16[2,24,80,2,8,80]{2,1,3,0,5,4:T(8,128)(2,1)} copy(bf16[2,24,80,2,8,80]{5,1,3,0,2,4:T(8,128)(2,1)} %bitcast.31) | data formatting | bytes 19660800 | tf_op jit(solution)/shard_map/all_to_all | solution.py:105
  854.6 25.0 %gather_fusion.1 = bf16[640,2,24,80,2]{3,2,4,1,0:T(8,128)(2,1)} fusion(bf16[2,24,80,2,640]{2,1,3,0,4:T(8,128)(2,1)} %bitcast.77, s32[1024]{0:T(1024)S(1)} %pad_clamp_fusion), kind=kCustom, calls=%fused_computation.1.clone | custom fusion | bytes 19663360 | tf_op jit(solution)/shard_map/jit(_take)/gather | solution.py:111
  879.5 14.0 %select_bitcast_fusion = bf16[2,24,80,2,640]{2,1,3,0,4:T(8,128)(2,1)} fusion(bf16[640,2,24,80,2]{3,2,4,1,0:T(8,128)(2,1)} %gather_fusion.1, pred[640]{0:T(1024)(128)(4,1)S(1)} %compare_and_fusion), kind=kLoop, calls=%fused_computation.8 | loop fusion | flops 4915200 | bytes 19661440 | tf_op jit(solution)/shard_map/jit(_take)/select_n | solution.py:111
  893.6 26.9 %copy.79 = bf16[2,24,80,2,640]{4,3,2,1,0:T(2,128)(2,1)} copy(bf16[2,24,80,2,640]{2,1,3,0,4:T(8,128)(2,1)} %select_bitcast_fusion) | data formatting | bytes 19660800 | tf_op jit(solution)/shard_map/jit(_take)/select_n | solution.py:111
  920.5 21.8 %dot_general.28 = bf16[2,24,80,1280]{3,2,1,0:T(8,128)(2,1)} reshape(bf16[2,24,80,2,640]{4,3,2,1,0:T(2,128)(2,1)} %copy.79) | data formatting | bytes 19660800 | tf_op jit(solution)/shard_map/dot_general | solution.py:112
  942.3 18.3 %fusion.33 = f32[2,24,80,1280]{3,2,1,0:T(8,128)} fusion(bf16[2,24,80,1280]{3,2,1,0:T(8,128)(2,1)} %dot_general.28, bf16[1280,1280,1,1]{1,0,3,2:T(8,128)(2,1)S(1)} %fusion.83), kind=kOutput, calls=%fused_computation.60 | convolution fusion | flops 12582912000 | bytes 32768000 | tf_op jit(solution)/shard_map/dot_general | solution.py:112
  (61 shorter events, 32.8 us)
Async XLA Ops:
  0.0 507.7 %copy-start = (bf16[96,96]{1,0:T(8,128)(2,1)S(1)}, bf16[96,96]{1,0:T(8,128)(2,1)}, u32[]{:S(2)}) copy-start(bf16[96,96]{1,0:T(8,128)(2,1)} %param.12) | copy-start | bytes 55300
  0.0 25.3 %copy-start.5 = (s32[1280]{0:T(1024)}, s32[1280]{0:T(1024)S(1)}, u32[]{:S(2)}) copy-start(s32[1280]{0:T(1024)S(1)} %get-tuple-element.14) | copy-start | bytes 15364
  0.0 25.3 %copy-start.7 = (s32[1280]{0:T(1024)}, s32[1280]{0:T(1024)S(1)}, u32[]{:S(2)}) copy-start(s32[1280]{0:T(1024)S(1)} %get-tuple-element.15) | copy-start | bytes 15364
  0.0 25.2 %copy-start.9 = (pred[1280]{0:T(1024)(128)(4,1)}, pred[1280]{0:T(1024)(128)(4,1)S(1)}, u32[]{:S(2)}) copy-start(pred[1280]{0:T(1024)(128)(4,1)S(1)} %get-tuple-element.16) | copy-start | bytes 3844
  0.1 25.2 %copy-start.11 = (pred[1280]{0:T(1024)(128)(4,1)}, pred[1280]{0:T(1024)(128)(4,1)S(1)}, u32[]{:S(2)}) copy-start(pred[1280]{0:T(1024)(128)(4,1)S(1)} %get-tuple-element.17) | copy-start | bytes 3844
  1.6 15.0 %copy-start.3 = (s32[320,2]{1,0:T(8,128)}, s32[320,2]{1,0:T(8,128)S(1)}, u32[]{:S(2)}) copy-start(s32[320,2]{1,0:T(8,128)S(1)} %copy.62) | copy-start | bytes 7684
  156.3 179.0 %all-to-all-start = ((bf16[2,24,80,2,640]{2,1,3,0,4:T(8,128)(2,1)}), bf16[2,24,80,2,640]{2,1,3,0,4:T(8,128)(2,1)}, u32[]{:S(2)}, u32[]{:S(2)}) async-start(bf16[2,24,80,2,640]{2,1,3,0,4:T(8,128)(2,1)} %select_bitcast_fusion.1), calls=%async_computation | async-start | bytes 31457280 | tf_op jit(solution)/shard_map/all_to_all | solution.py:59
  424.5 4.5 copy-start.2
  435.4 72.3 %copy-start.13 = (f32[96]{0:T(128)S(1)}, f32[96]{0:T(128)}, u32[]{:S(2)}) copy-start(f32[96]{0:T(128)} %param.13) | copy-start | bytes 1156
  438.8 68.9 %all-to-all-start.1 = ((bf16[24,4,12820]{2,0,1:T(8,128)(2,1)}), bf16[24,4,12820]{2,0,1:T(8,128)(2,1)S(1)}, u32[]{:S(2)}, u32[]{:S(2)}) async-start(bf16[24,4,12820]{2,0,1:T(8,128)(2,1)} %copy.70), calls=%async_computation.1 | async-start | bytes 4964352 | tf_op jit(solution)/shard_map/all_to_all | solution.py:78
  510.7 60.6 %all-to-all-start.2 = ((bf16[4,24,12820]{2,1,0:T(8,128)(2,1)}), bf16[4,24,12820]{2,1,0:T(8,128)(2,1)}, u32[]{:S(2)}, u32[]{:S(2)}) async-start(bf16[4,24,12820]{2,1,0:T(8,128)(2,1)} %bitcast.84), calls=%async_computation.2 | async-start | bytes 4964352 | tf_op jit(solution)/shard_map/all_to_all | solution.py:88
  642.1 6.0 copy-start.4
  642.1 10.4 %copy-start.6 = (s32[1280]{0:T(1024)S(1)}, s32[1280]{0:T(1024)}, u32[]{:S(2)}) copy-start(s32[1280]{0:T(1024)} %copy-done.5) | copy-start | bytes 15364
  642.1 10.4 %copy-start.8 = (s32[1280]{0:T(1024)S(1)}, s32[1280]{0:T(1024)}, u32[]{:S(2)}) copy-start(s32[1280]{0:T(1024)} %copy-done.7) | copy-start | bytes 15364
  642.1 10.4 %copy-start.10 = (pred[1280]{0:T(1024)(128)(4,1)S(1)}, pred[1280]{0:T(1024)(128)(4,1)}, u32[]{:S(2)}) copy-start(pred[1280]{0:T(1024)(128)(4,1)} %copy-done.9) | copy-start | bytes 3844
  642.1 10.4 %copy-start.12 = (pred[1280]{0:T(1024)(128)(4,1)S(1)}, pred[1280]{0:T(1024)(128)(4,1)}, u32[]{:S(2)}) copy-start(pred[1280]{0:T(1024)(128)(4,1)} %copy-done.11) | copy-start | bytes 3844
  642.2 178.7 %all-to-all-start.3 = ((bf16[2,24,640,2,80]{4,1,3,0,2:T(8,128)(2,1)}), bf16[2,24,640,2,80]{4,1,3,0,2:T(8,128)(2,1)}, u32[]{:S(2)}, u32[]{:S(2)}) async-start(bf16[2,24,640,2,80]{4,1,3,0,2:T(8,128)(2,1)} %copy.76), calls=%async_computation.3 | async-start | bytes 31457280 | tf_op jit(solution)/shard_map/all_to_all | solution.py:105
  942.3 18.3 %copy-start.1 = (bf16[96,96]{1,0:T(8,128)(2,1)S(1)}, bf16[96,96]{1,0:T(8,128)(2,1)}, u32[]{:S(2)}) copy-start(bf16[96,96]{1,0:T(8,128)(2,1)} %param.12) | copy-start | bytes 55300
where the time goes:
time: 973 us; the launch traced here: 961 us
  waiting for transfers between devices  416 us (43%)
  local copies, waits for them, and re-layouts  294 us (30%)
  other arithmetic  125 us (13%)
  matrix products  92.3 us (9%)
  starting transfers between devices  31.6 us (3%)
    all_to_all x1, waiting for transfers between devices, per_device(): lax.all_to_all(permuted, 'lat', split_axis=4, concat_axis=2, tiled=True)  173 us
    all_to_all x1, waiting for transfers between devices, per_device(): lax.all_to_all(synthesised, 'lat', split_axis=2, concat_axis=4, tiled=True)  138 us
    all_to_all x1, waiting for transfers between devices, per_device(): lax.all_to_all(padded, 'lev', split_axis=1, concat_axis=0, tiled=True)  52.9 us
    all_to_all x1, waiting for transfers between devices, per_device(): lax.all_to_all(solved_columns.astype(jnp.bfloat16), 'lev', split_axis=0,...  52.7 us
    reshape x2, local copies, waits for them, and re-layouts, per_device(): fourier_local.astype(jnp.bfloat16)  45.2 us
    all_to_all x1, local copies, waits for them, and re-layouts, per_device(): lax.all_to_all(synthesised, 'lat', split_axis=2, concat_axis=4, tiled=True)  33.7 us
    dot_general x1, other arithmetic, per_device(): jnp.dot(natural.reshape(-1, 2 * wave_count), inverse, preferred_element_t...  30 us
    dot_general x1, matrix products, per_device(): jnp.einsum('slj,fvlcsh->sfvchj', legendre, grouped, preferred_element_typ...  29.7 us
  transfers between devices with their start and end apart: 4, of which 4 were waited for; matrix products, arithmetic and copies ran while one was open for 4% of the time, Pallas kernels for 0%

commit v1 on v0

--- a/solution.py
+++ b/solution.py
@@ -56,7 +56,25 @@
     )
     column_order = jnp.stack([pair_order, wave_count - 1 - pair_order], axis=1).reshape(-1)
     permuted = jnp.take(fourier_local, column_order, axis=4)
-    received_bands = lax.all_to_all(permuted, "lat", split_axis=4, concat_axis=2, tiled=True)
+    high = lax.psum(1, "lat")
+    y_new = lax.axis_index("lat")
+    item_now, mid_arr = (high, y_new)
+    f_now = permuted.shape[4] // item_now
+    side_arr = list(permuted.shape)
+    side_arr[4] = f_now
+    outer = side_arr[2]
+    side_arr[2] = outer * item_now
+    received_bands = jnp.zeros(side_arr, permuted.dtype)
+    for ii in range(item_now):
+        work_now = lax.dynamic_slice_in_dim(permuted, (mid_arr ^ ii) * f_now, f_now, axis=4)
+        if ii:
+            store = []
+            for j in range(item_now):
+                store.append((j, j ^ ii))
+            work_now = lax.ppermute(work_now, axis_name="lat", perm=store)
+        received_bands = lax.dynamic_update_slice_in_dim(
+            received_bands, work_now, (mid_arr ^ ii) * outer, axis=2
+        )
     grouped = received_bands.reshape(fields, levels, lat_count, 2, slot_count, 2)
     band_index = lax.axis_index("lat")
     local_waves = lax.dynamic_slice_in_dim(pair_order, band_index * slot_count, slot_count)

time: 973 us -> 1260 us (1.29)
  local copies, waits for them, and re-layouts: 294 us -> 723 us
  waiting for transfers between devices: 416 us -> 288 us
    dynamic_update_slice x0 -> x8, local copies, waits for them, and re-layouts: none -> 456 us  [per_device(): lax.dynamic_update_slice_in_dim(received_bands, work_now, (mid_arr ^ ii)...]
    all_to_all x1 -> x0, waiting for transfers between devices: 173 us -> none  [per_device(): lax.all_to_all(permuted, 'lat', split_axis=4, concat_axis=2, tiled=True)]
    ppermute x0 -> x7, waiting for transfers between devices: none -> 38.8 us  [per_device(): work_now = lax.ppermute(work_now, axis_name='lat', perm=store)]
    all_to_all x1 -> x0, local copies, waits for them, and re-layouts: 27.2 us -> none  [per_device(): lax.all_to_all(permuted, 'lat', split_axis=4, concat_axis=2, tiled=True)]
    reshape x1 -> x0, local copies, waits for them, and re-layouts: 23.1 us -> none  [per_device(): received_bands.reshape(fields, levels, lat_count, 2, slot_count, 2)]
    ppermute x0 -> x7, local copies, waits for them, and re-layouts: none -> 13.2 us  [per_device(): work_now = lax.ppermute(work_now, axis_name='lat', perm=store)]
  transfers between devices with their start and end apart: 4 -> 10, of which waited for: 4 -> 4; matrix products, arithmetic and copies ran while one was open for 4% -> 36% of each run, Pallas kernels for 0% -> 0%
where the time goes in v1:
time: 1260 us; the launch traced here: 1250 us
  local copies, waits for them, and re-layouts  723 us (57%)
  waiting for transfers between devices  288 us (23%)
  other arithmetic  120 us (10%)
  matrix products  92.3 us (7%)
  starting transfers between devices  25.3 us (2%)
    dynamic_update_slice x8, local copies, waits for them, and re-layouts, per_device(): lax.dynamic_update_slice_in_dim(received_bands, work_now, (mid_arr ^ ii)...  456 us
    all_to_all x1, waiting for transfers between devices, per_device(): lax.all_to_all(synthesised, 'lat', split_axis=2, concat_axis=4, tiled=True)  138 us
    all_to_all x1, waiting for transfers between devices, per_device(): lax.all_to_all(padded, 'lev', split_axis=1, concat_axis=0, tiled=True)  57.2 us
    all_to_all x1, waiting for transfers between devices, per_device(): lax.all_to_all(solved_columns.astype(jnp.bfloat16), 'lev', split_axis=0,...  53.6 us
    reshape x2, local copies, waits for them, and re-layouts, per_device(): fourier_local.astype(jnp.bfloat16)  45.2 us
    ppermute x7, waiting for transfers between devices, per_device(): work_now = lax.ppermute(work_now, axis_name='lat', perm=store)  38.8 us
    all_to_all x1, local copies, waits for them, and re-layouts, per_device(): lax.all_to_all(synthesised, 'lat', split_axis=2, concat_axis=4, tiled=True)  33.7 us
    dot_general x1, other arithmetic, per_device(): jnp.dot(natural.reshape(-1, 2 * wave_count), inverse, preferred_element_t...  30 us
  transfers between devices with their start and end apart: 10, of which 4 were waited for; matrix products, arithmetic and copies ran while one was open for 36% of the time, Pallas kernels for 0%

profile of v1, /device:TPU:0, one launch (start us, length us, event | category | flops | bytes accessed | tf_op | source)
XLA Modules:
  0.0 1249.8 jit_solution(11737598205173073039)
XLA Ops:
  1.8 14.9 %fusion.9 = (bf16[1,24,80,1280]{3,2,1,0:T(8,128)(2,1)}, bf16[1,24,80,1280]{3,2,1,0:T(8,128)(2,1)}) fusion(f32[2,24,80,1280]{3,2,1,0:T(8,128)} %param.8, bf16[2,24,80,1280]{3,2,1,0:T(8,128)(2,1)} %param.9), kind=kLoop, calls=%fused_computation.24 | loop fusion | flops 24576000 | bytes 39321600 | tf_op jit(solution)/shard_map/convert.8
  16.6 8.6 pad_maximum_fusion.1
  25.3 27.6 %multiply_convert_fusion.4 = bf16[1280,1280]{1,0:T(8,128)(2,1)S(1)} fusion(s32[1280]{0:T(1024)S(1)} %get-tuple-element.22, s32[1280]{0:T(1024)S(1)} %get-tuple-element.23, pred[1280]{0:T(1024)(128)(4,1)S(1)} %get-tuple-element.25, pred[1280]{0:T(1024)(128)(4,1)S(1)} %get-tuple-element.24), kind=kLoop, calls=%fused_computation.46.clone.clone.1 | loop fusion | flops 22937600 | bytes 3289600 | tf_op jit(solution)/shard_map/dot_general | solution.py:51
  52.9 19.0 %convolution_convert_fusion.1 = bf16[3840,1280]{1,0:T(8,128)(2,1)} fusion(bf16[3840,1280]{1,0:T(8,128)(2,1)} %bitcast.75, bf16[1280,1280]{1,0:T(8,128)(2,1)S(1)} %multiply_convert_fusion.4), kind=kOutput, calls=%fused_computation.13 | convolution fusion | flops 12587827200 | bytes 22937600 | tf_op jit(solution)/shard_map/dot_general | solution.py:51
  71.8 19.3 %reshape.232 = bf16[2,24,80,2,640]{4,3,2,1,0:T(2,128)(2,1)} reshape(bf16[3840,1280]{1,0:T(8,128)(2,1)} %convolution_convert_fusion.1) | data formatting | bytes 19660800 | tf_op jit(solution)/shard_map/reshape | solution.py:54
  91.1 25.9 %copy.85 = bf16[2,24,80,2,640]{2,1,3,0,4:T(8,128)(2,1)} copy(bf16[2,24,80,2,640]{4,3,2,1,0:T(2,128)(2,1)} %reshape.232) | data formatting | bytes 19660800 | tf_op jit(solution)/shard_map/reshape | solution.py:54
  117.1 25.1 %gather_fusion = bf16[640,2,24,80,2]{3,2,4,1,0:T(8,128)(2,1)} fusion(bf16[2,24,80,2,640]{2,1,3,0,4:T(8,128)(2,1)} %copy.85, s32[1024]{0:T(1024)S(1)} %pad_clamp_fusion.1), kind=kCustom, calls=%fused_computation.clone | custom fusion | bytes 19663360 | tf_op jit(solution)/shard_map/jit(_take)/gather | solution.py:58
  142.2 8.8 select_bitcast_fusion.1
  163.5 38.7 %collective-permute-done.1 = bf16[2,24,80,2,80]{2,1,3,0,4:T(8,128)(2,1)S(1)} collective-permute-done((bf16[2,24,80,2,80]{2,1,3,0,4:T(8,128)(2,1)S(1)}, bf16[2,24,80,2,80]{2,1,3,0,4:T(8,128)(2,1)S(1)}, u32[]{:S(2)}, u32[]{:S(2)}) %collective-permute-start.1) | collective-permute-done | bytes 1228832 | tf_op jit(solution)/shard_map/ppermute | solution.py:74
  209.1 23.1 %dynamic_update_slice.24 = bf16[2,24,640,2,80]{2,1,4,3,0:T(8,128)(2,1)} dynamic-update-slice(bf16[2,24,640,2,80]{2,1,4,3,0:T(8,128)(2,1)} %broadcast_in_dim.63, bf16[2,24,80,2,80]{2,1,4,3,0:T(8,128)(2,1)S(1)} %copy.86, s32[]{:T(128)} %constant.30.clone.1, s32[]{:T(128)} %constant.30.clone.1, s32[]{:T(128)S(6)} %select_n.127, s32[]{:T(128)} %constant.30.clone.1, s32[]{:T(128)} %constant.30.clone.1) | dynamic-update-slice | bytes 2457604 | tf_op jit(solution)/shard_map/dynamic_update_slice | solution.py:75
  235.0 61.9 %dynamic_update_slice.25 = bf16[2,24,640,2,80]{2,1,4,3,0:T(8,128)(2,1)} dynamic-update-slice(bf16[2,24,640,2,80]{2,1,4,3,0:T(8,128)(2,1)} %dynamic_update_slice.24, bf16[2,24,80,2,80]{2,1,4,3,0:T(8,128)(2,1)S(1)} %copy.87, s32[]{:T(128)} %constant.30.clone.1, s32[]{:T(128)} %constant.30.clone.1, s32[]{:T(128)S(6)} %select_n.128, s32[]{:T(128)} %constant.30.clone.1, s32[]{:T(128)} %constant.30.clone.1) | dynamic-update-slice | bytes 2457604 | tf_op jit(solution)/shard_map/dynamic_update_slice | solution.py:75
  298.8 61.9 %dynamic_update_slice.26 = bf16[2,24,640,2,80]{2,1,4,3,0:T(8,128)(2,1)} dynamic-update-slice(bf16[2,24,640,2,80]{2,1,4,3,0:T(8,128)(2,1)} %dynamic_update_slice.25, bf16[2,24,80,2,80]{2,1,4,3,0:T(8,128)(2,1)S(1)} %copy.88, s32[]{:T(128)} %constant.30.clone.1, s32[]{:T(128)} %constant.30.clone.1, s32[]{:T(128)S(6)} %select_n.129, s32[]{:T(128)} %constant.30.clone.1, s32[]{:T(128)} %constant.30.clone.1) | dynamic-update-slice | bytes 2457604 | tf_op jit(solution)/shard_map/dynamic_update_slice | solution.py:75
  362.5 62.3 %dynamic_update_slice.27 = bf16[2,24,640,2,80]{2,1,4,3,0:T(8,128)(2,1)} dynamic-update-slice(bf16[2,24,640,2,80]{2,1,4,3,0:T(8,128)(2,1)} %dynamic_update_slice.26, bf16[2,24,80,2,80]{2,1,4,3,0:T(8,128)(2,1)S(1)} %copy.89, s32[]{:T(128)} %constant.30.clone.1, s32[]{:T(128)} %constant.30.clone.1, s32[]{:T(128)S(6)} %select_n.130, s32[]{:T(128)} %constant.30.clone.1, s32[]{:T(128)} %constant.30.clone.1) | dynamic-update-slice | bytes 2457604 | tf_op jit(solution)/shard_map/dynamic_update_slice | solution.py:75
  426.7 61.9 %dynamic_update_slice.28 = bf16[2,24,640,2,80]{2,1,4,3,0:T(8,128)(2,1)} dynamic-update-slice(bf16[2,24,640,2,80]{2,1,4,3,0:T(8,128)(2,1)} %dynamic_update_slice.27, bf16[2,24,80,2,80]{2,1,4,3,0:T(8,128)(2,1)S(1)} %copy.90, s32[]{:T(128)} %constant.30.clone.1, s32[]{:T(128)} %constant.30.clone.1, s32[]{:T(128)S(6)} %select_n.131, s32[]{:T(128)} %constant.30.clone.1, s32[]{:T(128)} %constant.30.clone.1) | dynamic-update-slice | bytes 2457604 | tf_op jit(solution)/shard_map/dynamic_update_slice | solution.py:75
  490.5 61.9 %dynamic_update_slice.29 = bf16[2,24,640,2,80]{2,1,4,3,0:T(8,128)(2,1)} dynamic-update-slice(bf16[2,24,640,2,80]{2,1,4,3,0:T(8,128)(2,1)} %dynamic_update_slice.28, bf16[2,24,80,2,80]{2,1,4,3,0:T(8,128)(2,1)S(1)} %copy.91, s32[]{:T(128)} %constant.30.clone.1, s32[]{:T(128)} %constant.30.clone.1, s32[]{:T(128)S(6)} %select_n.132, s32[]{:T(128)} %constant.30.clone.1, s32[]{:T(128)} %constant.30.clone.1) | dynamic-update-slice | bytes 2457604 | tf_op jit(solution)/shard_map/dynamic_update_slice | solution.py:75
  554.3 61.9 %dynamic_update_slice.30 = bf16[2,24,640,2,80]{2,1,4,3,0:T(8,128)(2,1)} dynamic-update-slice(bf16[2,24,640,2,80]{2,1,4,3,0:T(8,128)(2,1)} %dynamic_update_slice.29, bf16[2,24,80,2,80]{2,1,4,3,0:T(8,128)(2,1)S(1)} %copy.92, s32[]{:T(128)} %constant.30.clone.1, s32[]{:T(128)} %constant.30.clone.1, s32[]{:T(128)S(6)} %select_n.133, s32[]{:T(128)} %constant.30.clone.1, s32[]{:T(128)} %constant.30.clone.1) | dynamic-update-slice | bytes 2457604 | tf_op jit(solution)/shard_map/dynamic_update_slice | solution.py:75
  618.1 61.3 %dynamic_update_slice.31 = bf16[2,24,640,2,80]{2,1,4,3,0:T(8,128)(2,1)} dynamic-update-slice(bf16[2,24,640,2,80]{2,1,4,3,0:T(8,128)(2,1)} %dynamic_update_slice.30, bf16[2,24,80,2,80]{2,1,4,3,0:T(8,128)(2,1)S(1)} %copy.93, s32[]{:T(128)} %constant.30.clone.1, s32[]{:T(128)} %constant.30.clone.1, s32[]{:T(128)S(6)} %select_n.134, s32[]{:T(128)} %constant.30.clone.1, s32[]{:T(128)} %constant.30.clone.1) | dynamic-update-slice | bytes 2457604 | tf_op jit(solution)/shard_map/dynamic_update_slice | solution.py:75
  679.4 29.7 %fusion.2 = f32[40,2,24,2,2,641]{5,2,4,3,1,0:T(8,128)} fusion(bf16[40,640,641,1,1,1]{1,0,2,5,4,3:T(8,128)(2,1)} %bitcast.72, bf16[2,24,640,2,40,2]{2,1,5,4,3,0:T(8,128)(2,1)} %bitcast.71), kind=kOutput, calls=%fused_computation.5 | convolution fusion | flops 6301286400 | bytes 62341120 | tf_op jit(solution)/shard_map/slj,fvlcsh->sfvchj/dot_general | solution.py:82
  709.1 9.1 fusion.6
  738.1 57.2 %all-to-all-done = bf16[24,4,12820]{2,0,1:T(8,128)(2,1)S(1)} async-done(((bf16[24,4,12820]{2,0,1:T(8,128)(2,1)}), bf16[24,4,12820]{2,0,1:T(8,128)(2,1)S(1)}, u32[]{:S(2)}, u32[]{:S(2)}) %all-to-all-start) | async-done | bytes 2461472 | tf_op jit(solution)/shard_map/all_to_all | solution.py:96
  806.4 53.6 %all-to-all-done.1 = bf16[4,24,12820]{2,1,0:T(8,128)(2,1)} async-done(((bf16[4,24,12820]{2,1,0:T(8,128)(2,1)}), bf16[4,24,12820]{2,1,0:T(8,128)(2,1)}, u32[]{:S(2)}, u32[]{:S(2)}) %all-to-all-start.1) | async-done | bytes 2461472 | tf_op jit(solution)/shard_map/all_to_all | solution.py:106
  864.2 10.8 convert_element_type.92
  880.0 22.3 %convert_bitcast_fusion = bf16[2,24,640,2,40,2]{2,1,5,3,0,4:T(8,128)(2,1)} fusion(bf16[40,640,641,1,1,1]{1,0,2,5,4,3:T(8,128)(2,1)} %bitcast.73, bf16[40,2,24,2,1,641]{5,2,3,0,4,1:T(8,128)(2,1)S(1)} %get-tuple-element.19, bf16[40,2,24,2,1,641]{5,2,3,0,4,1:T(8,128)(2,1)S(1)} %get-tuple-element.18), kind=kOutput, calls=%fused_computation.30 | convolution fusion | flops 6311124480 | bytes 52495360 | tf_op jit(solution)/shard_map/slj,sfvchj->fvlcsh/dot_general | solution.py:117
  910.7 20.1 %copy.104 = bf16[2,24,640,2,80]{4,1,3,0,2:T(8,128)(2,1)} copy(bf16[2,24,640,2,80]{2,1,4,3,0:T(8,128)(2,1)} %bitcast.70) | data formatting | bytes 19660800 | tf_op jit(solution)/shard_map/reshape | solution.py:120
  941.2 30.0 %fusion.83 = bf16[1280,1280,1,1]{1,0,3,2:T(8,128)(2,1)S(1)} fusion(s32[1280]{0:T(1024)S(1)} %copy-done.8, s32[1280]{0:T(1024)S(1)} %copy-done.10, pred[1280]{0:T(1024)(128)(4,1)S(1)} %copy-done.14, pred[1280]{0:T(1024)(128)(4,1)S(1)} %copy-done.12), kind=kLoop, calls=%fused_computation.58.clone.clone.1 | loop fusion | flops 27852800 | bytes 3289600 | tf_op jit(solution)/shard_map/dot_general | solution.py:130
  971.2 138.4 %all-to-all-done.2 = bf16[2,24,640,2,80]{4,1,3,0,2:T(8,128)(2,1)} async-done(((bf16[2,24,640,2,80]{4,1,3,0,2:T(8,128)(2,1)}), bf16[2,24,640,2,80]{4,1,3,0,2:T(8,128)(2,1)}, u32[]{:S(2)}, u32[]{:S(2)}) %all-to-all-start.2) | async-done | bytes 9830432 | tf_op jit(solution)/shard_map/all_to_all | solution.py:123
  1109.5 33.7 %copy.115 = bf16[2,24,80,2,8,80]{2,1,3,0,5,4:T(8,128)(2,1)} copy(bf16[2,24,80,2,8,80]{5,1,3,0,2,4:T(8,128)(2,1)} %bitcast.30) | data formatting | bytes 19660800 | tf_op jit(solution)/shard_map/all_to_all | solution.py:123
  1143.3 25.0 %gather_fusion.1 = bf16[640,2,24,80,2]{3,2,4,1,0:T(8,128)(2,1)} fusion(bf16[2,24,80,2,640]{2,1,3,0,4:T(8,128)(2,1)} %bitcast.69, s32[1024]{0:T(1024)S(1)} %pad_clamp_fusion), kind=kCustom, calls=%fused_computation.1.clone | custom fusion | bytes 19663360 | tf_op jit(solution)/shard_map/jit(_take)/gather | solution.py:129
  1168.2 14.0 %select_bitcast_fusion = bf16[2,24,80,2,640]{2,1,3,0,4:T(8,128)(2,1)} fusion(bf16[640,2,24,80,2]{3,2,4,1,0:T(8,128)(2,1)} %gather_fusion.1, pred[640]{0:T(1024)(128)(4,1)S(1)} %compare_and_fusion), kind=kLoop, calls=%fused_computation.7 | loop fusion | flops 4915200 | bytes 19661440 | tf_op jit(solution)/shard_map/jit(_take)/select_n | solution.py:129
  1182.2 27.0 %copy.107 = bf16[2,24,80,2,640]{4,3,2,1,0:T(2,128)(2,1)} copy(bf16[2,24,80,2,640]{2,1,3,0,4:T(8,128)(2,1)} %select_bitcast_fusion) | data formatting | bytes 19660800 | tf_op jit(solution)/shard_map/jit(_take)/select_n | solution.py:129
  1209.2 21.8 %dot_general.28 = bf16[2,24,80,1280]{3,2,1,0:T(8,128)(2,1)} reshape(bf16[2,24,80,2,640]{4,3,2,1,0:T(2,128)(2,1)} %copy.107) | data formatting | bytes 19660800 | tf_op jit(solution)/shard_map/dot_general | solution.py:130
  1231.0 18.3 %fusion.33 = f32[2,24,80,1280]{3,2,1,0:T(8,128)} fusion(bf16[2,24,80,1280]{3,2,1,0:T(8,128)(2,1)} %dot_general.28, bf16[1280,1280,1,1]{1,0,3,2:T(8,128)(2,1)S(1)} %fusion.83), kind=kOutput, calls=%fused_computation.59 | convolution fusion | flops 12582912000 | bytes 32768000 | tf_op jit(solution)/shard_map/dot_general | solution.py:130
  (93 shorter events, 93.9 us)
Async XLA Ops:
  0.0 795.3 %copy-start = (bf16[96,96]{1,0:T(8,128)(2,1)S(1)}, bf16[96,96]{1,0:T(8,128)(2,1)}, u32[]{:S(2)}) copy-start(bf16[96,96]{1,0:T(8,128)(2,1)} %param.12) | copy-start | bytes 55300
  0.0 25.3 %copy-start.7 = (s32[1280]{0:T(1024)}, s32[1280]{0:T(1024)S(1)}, u32[]{:S(2)}) copy-start(s32[1280]{0:T(1024)S(1)} %get-tuple-element.22) | copy-start | bytes 15364
  0.0 25.3 %copy-start.9 = (s32[1280]{0:T(1024)}, s32[1280]{0:T(1024)S(1)}, u32[]{:S(2)}) copy-start(s32[1280]{0:T(1024)S(1)} %get-tuple-element.23) | copy-start | bytes 15364
  0.0 25.2 %copy-start.11 = (pred[1280]{0:T(1024)(128)(4,1)}, pred[1280]{0:T(1024)(128)(4,1)S(1)}, u32[]{:S(2)}) copy-start(pred[1280]{0:T(1024)(128)(4,1)S(1)} %get-tuple-element.24) | copy-start | bytes 3844
  0.1 25.2 %copy-start.13 = (pred[1280]{0:T(1024)(128)(4,1)}, pred[1280]{0:T(1024)(128)(4,1)S(1)}, u32[]{:S(2)}) copy-start(pred[1280]{0:T(1024)(128)(4,1)S(1)} %get-tuple-element.25) | copy-start | bytes 3844
  1.6 15.0 %copy-start.5 = (s32[320,2]{1,0:T(8,128)}, s32[320,2]{1,0:T(8,128)S(1)}, u32[]{:S(2)}) copy-start(s32[320,2]{1,0:T(8,128)S(1)} %copy.83) | copy-start | bytes 7684
  155.6 4.9 collective-permute-start
  156.1 46.2 %collective-permute-start.1 = (bf16[2,24,80,2,80]{2,1,3,0,4:T(8,128)(2,1)S(1)}, bf16[2,24,80,2,80]{2,1,3,0,4:T(8,128)(2,1)S(1)}, u32[]{:S(2)}, u32[]{:S(2)}) collective-permute-start(bf16[2,24,80,2,80]{2,1,3,0,4:T(8,128)(2,1)S(1)} %get-tuple-element.15), channel_id=1, source_target_pairs={{0,8},{4,12},{8,0},{12,4},{16,24},{20,28},{24,16},{28,20},{1,9},{5... | collective-permute-start | bytes 3686408 | tf_op jit(solution)/shard_map/ppermute | solution.py:74
  158.6 202.1 %collective-permute-start.2 = (bf16[2,24,80,2,80]{2,1,3,0,4:T(8,128)(2,1)}, bf16[2,24,80,2,80]{2,1,3,0,4:T(8,128)(2,1)}, u32[]{:S(2)}, u32[]{:S(2)}) collective-permute-start(bf16[2,24,80,2,80]{2,1,3,0,4:T(8,128)(2,1)} %get-tuple-element.14), channel_id=1, source_target_pairs={{0,12},{4,8},{8,4},{12,0},{16,28},{20,24},{24,20},{28,16},{1,13},{... | collective-permute-start | bytes 3686408 | tf_op jit(solution)/shard_map/ppermute | solution.py:74
  158.7 266.1 %collective-permute-start.3 = (bf16[2,24,80,2,80]{2,1,3,0,4:T(8,128)(2,1)}, bf16[2,24,80,2,80]{2,1,3,0,4:T(8,128)(2,1)}, u32[]{:S(2)}, u32[]{:S(2)}) collective-permute-start(bf16[2,24,80,2,80]{2,1,3,0,4:T(8,128)(2,1)} %get-tuple-element.13), channel_id=1, source_target_pairs={{0,16},{4,20},{8,24},{12,28},{16,0},{20,4},{24,8},{28,12},{1,17},{... | collective-permute-start | bytes 3686408 | tf_op jit(solution)/shard_map/ppermute | solution.py:74
  160.5 328.1 %collective-permute-start.4 = (bf16[2,24,80,2,80]{2,1,3,0,4:T(8,128)(2,1)}, bf16[2,24,80,2,80]{2,1,3,0,4:T(8,128)(2,1)}, u32[]{:S(2)}, u32[]{:S(2)}) collective-permute-start(bf16[2,24,80,2,80]{2,1,3,0,4:T(8,128)(2,1)} %get-tuple-element.12), channel_id=1, source_target_pairs={{0,20},{4,16},{8,28},{12,24},{16,4},{20,0},{24,12},{28,8},{1,21},{... | collective-permute-start | bytes 3686408 | tf_op jit(solution)/shard_map/ppermute | solution.py:74
  160.5 43.7 %copy-start.4 = (bf16[2,24,80,2,80]{2,1,3,0,4:T(8,128)(2,1)}, bf16[2,24,80,2,80]{2,1,3,0,4:T(8,128)(2,1)S(1)}, u32[]{:S(2)}) copy-start(bf16[2,24,80,2,80]{2,1,3,0,4:T(8,128)(2,1)S(1)} %collective-permute-done) | copy-start | bytes 3686404
  160.5 391.9 %collective-permute-start.5 = (bf16[2,24,80,2,80]{2,1,3,0,4:T(8,128)(2,1)}, bf16[2,24,80,2,80]{2,1,3,0,4:T(8,128)(2,1)}, u32[]{:S(2)}, u32[]{:S(2)}) collective-permute-start(bf16[2,24,80,2,80]{2,1,3,0,4:T(8,128)(2,1)} %get-tuple-element.11), channel_id=1, source_target_pairs={{0,24},{4,28},{8,16},{12,20},{16,8},{20,12},{24,0},{28,4},{1,25},{... | collective-permute-start | bytes 3686408 | tf_op jit(solution)/shard_map/ppermute | solution.py:74
  202.3 1.9 copy-start.3
  202.3 413.9 %collective-permute-start.6 = (bf16[2,24,80,2,80]{2,1,3,0,4:T(8,128)(2,1)}, bf16[2,24,80,2,80]{2,1,3,0,4:T(8,128)(2,1)}, u32[]{:S(2)}, u32[]{:S(2)}) collective-permute-start(bf16[2,24,80,2,80]{2,1,3,0,4:T(8,128)(2,1)} %get-tuple-element.10), channel_id=1, source_target_pairs={{0,28},{4,24},{8,20},{12,16},{16,12},{20,8},{24,4},{28,0},{1,29},{... | collective-permute-start | bytes 3686408 | tf_op jit(solution)/shard_map/ppermute | solution.py:74
  718.2 4.5 copy-start.2
  729.1 66.1 %copy-start.15 = (f32[96]{0:T(128)S(1)}, f32[96]{0:T(128)}, u32[]{:S(2)}) copy-start(f32[96]{0:T(128)} %param.13) | copy-start | bytes 1156
  732.6 62.7 %all-to-all-start = ((bf16[24,4,12820]{2,0,1:T(8,128)(2,1)}), bf16[24,4,12820]{2,0,1:T(8,128)(2,1)S(1)}, u32[]{:S(2)}, u32[]{:S(2)}) async-start(bf16[24,4,12820]{2,0,1:T(8,128)(2,1)} %copy.98), calls=%async_computation | async-start | bytes 4964352 | tf_op jit(solution)/shard_map/all_to_all | solution.py:96
  798.3 61.7 %all-to-all-start.1 = ((bf16[4,24,12820]{2,1,0:T(8,128)(2,1)}), bf16[4,24,12820]{2,1,0:T(8,128)(2,1)}, u32[]{:S(2)}, u32[]{:S(2)}) async-start(bf16[4,24,12820]{2,1,0:T(8,128)(2,1)} %bitcast.77), calls=%async_computation.1 | async-start | bytes 4964352 | tf_op jit(solution)/shard_map/all_to_all | solution.py:106
  930.8 6.0 copy-start.6
  930.8 10.4 copy-start.8
  930.8 10.4 copy-start.10
  930.8 10.4 copy-start.12
  930.8 10.4 copy-start.14
  930.8 178.7 %all-to-all-start.2 = ((bf16[2,24,640,2,80]{4,1,3,0,2:T(8,128)(2,1)}), bf16[2,24,640,2,80]{4,1,3,0,2:T(8,128)(2,1)}, u32[]{:S(2)}, u32[]{:S(2)}) async-start(bf16[2,24,640,2,80]{4,1,3,0,2:T(8,128)(2,1)} %copy.104), calls=%async_computation.2 | async-start | bytes 31457280 | tf_op jit(solution)/shard_map/all_to_all | solution.py:123
  1231.0 18.3 %copy-start.1 = (bf16[96,96]{1,0:T(8,128)(2,1)S(1)}, bf16[96,96]{1,0:T(8,128)(2,1)}, u32[]{:S(2)}) copy-start(bf16[96,96]{1,0:T(8,128)(2,1)} %param.12) | copy-start | bytes 55300
